TPU v7x, 32 devices: a whole 2x2x4 slice. The times are simulated.
32 devices in a mesh: gz: 4 (over y, x), gy: 8 (over z, core).
Axes of the slice: x: 2, y: 2, z: 4, core: 2. Of those that a mesh axis runs over, the one named last changes fastest.
Arguments:
- fixed: float32 [128, 512, 256], P('gz', 'gy'), may hold values from -6 to 6
- moving: float32 [128, 512, 256], P('gz', 'gy'), may hold values from -6 to 6
Outputs:
- update: float32 [3, 16, 64, 32], P(None, 'gz', 'gy')
- residual: float32 [3, 16, 64, 32], P(None, 'gz', 'gy')
All inputs are finite; a program needn't handle non-finite values.
Results may differ from a plain program's by a relative error of at most 0.0031.
Values sent between devices are 32-bit elements; how exact they have to be, the bound alone decides.
No kernel may reach another device: no remote copies, remote signals or barrier semaphores. Data moves between devices by JAX's collectives and lax.ppermute only.
A program may use at most 64 MiB of HBM per device.

v0:
```python
import jax
import jax.numpy as jnp
from jax import lax
from jax.sharding import PartitionSpec as P

SPACING = 8
ITERS = 2
damping_weight = 8.0


def from_behind(value, axis, steps):
    count = lax.axis_size(axis)
    initial, last = (max(0, -steps), min(count, count - steps))
    return lax.ppermute(value, axis, [(source, source + steps) for source in range(initial, last)])


def padded_2(cells, sides, width):
    for axis, dim in sides:
        count = lax.axis_size(axis)
        ends = count - 1
        head = lax.slice_in_dim(cells, 0, width, axis=dim)
        tail = lax.slice_in_dim(cells, cells.shape[dim] - width, cells.shape[dim], axis=dim)
        cells = jnp.concatenate(
            [
                lax.ppermute(tail, axis, [(i, (i + 1) % count) for i in range(ends)]),
                cells,
                lax.ppermute(head, axis, [((i + 1) % count, i) for i in range(ends)]),
            ],
            axis=dim,
        )
    return cells


def basis_matrix(count, columns, offset):
    voxel = jnp.arange(count, dtype=jnp.int32)
    cell = voxel // SPACING
    frac = ((voxel % SPACING).astype(jnp.float32) + 0.5) / SPACING
    other = 1.0 - frac
    weights = (
        other**3 / 6.0,
        (3.0 * frac**3 - 6.0 * frac**2 + 4.0) / 6.0,
        (-3.0 * frac**3 + 3.0 * frac**2 + 3.0 * frac + 1.0) / 6.0,
        frac**3 / 6.0,
    )
    index = jnp.arange(columns, dtype=jnp.int32)
    matrix = jnp.zeros((count, columns), jnp.float32)
    for tap in range(4):
        match = index[None, :] == (cell - 1 + tap + offset)[:, None]
        matrix = matrix + jnp.where(match, weights[tap][:, None], jnp.float32(0.0))
    return matrix


def decode(control, along_z, along_y, along_x):
    hp = lax.Precision.HIGHEST
    inner = jnp.einsum("cabe,xe->cabx", control, along_x, precision=hp)
    inner = jnp.einsum("yb,cabx->cayx", along_y, inner, precision=hp)
    return jnp.einsum("za,cayx->czyx", along_z, inner, precision=hp)


def encode(volume, along_z, along_y, along_x):
    hp = lax.Precision.HIGHEST
    inner = jnp.einsum("za,czyx->cayx", along_z, volume, precision=hp)
    inner = jnp.einsum("yb,cayx->cabx", along_y, inner, precision=hp)
    return jnp.einsum("xe,cabx->cabe", along_x, inner, precision=hp)


def derivative(padded, axis):
    length = padded.shape[axis] - 6

    def part(shift_by):
        return lax.slice_in_dim(padded, 3 + shift_by, 3 + shift_by + length, axis=axis)

    return (45.0 * (part(1) - part(-1)) - 9.0 * (part(2) - part(-2)) + (part(3) - part(-3))) / 60.0


def fold_rims(extended):
    depth = extended.shape[1] - 4
    from_above = from_behind(extended[:, 0:2], "gz", -1)
    from_below = from_behind(extended[:, depth + 2 : depth + 4], "gz", 1)
    core = extended[:, 2 : depth + 2]
    core = core.at[:, depth - 2 :].add(from_above).at[:, :2].add(from_below)
    width = core.shape[2] - 4
    from_right = from_behind(core[:, :, 0:2], "gy", -1)
    from_left = from_behind(core[:, :, width + 2 : width + 4], "gy", 1)
    inner = core[:, :, 2 : width + 2]
    return inner.at[:, :, width - 2 :].add(from_right).at[:, :, :2].add(from_left)


def two_products(residual, image):
    return lax.psum((jnp.sum(residual * residual), jnp.sum(residual * image)), ("gz", "gy"))


def shards(fixed, moving):
    slab_z, slab_y, extent = fixed.shape
    pair = jnp.stack([fixed, moving])
    framed = padded_2(pair, (("gz", 1), ("gy", 2)), 3)
    framed = 0.5 * (framed[0] + framed[1])
    framed = jnp.pad(framed, ((0, 0), (0, 0), (3, 3)))
    gradient = jnp.stack(
        [
            derivative(framed[:, 3:-3, 3:-3], 0),
            derivative(framed[3:-3, :, 3:-3], 1),
            derivative(framed[3:-3, 3:-3, :], 2),
        ]
    ).astype(jnp.bfloat16)
    mismatch = moving - fixed
    ctrl_z = slab_z // SPACING
    ctrl_y = slab_y // SPACING
    ctrl_x = extent // SPACING
    along_z = basis_matrix(slab_z, ctrl_z + 4, 2)
    along_y = basis_matrix(slab_y, ctrl_y + 4, 2)
    along_x = basis_matrix(extent, ctrl_x, 0)
    slopes = gradient.astype(jnp.float32)

    def operate(control):
        extended = padded_2(control, (("gz", 1), ("gy", 2)), 2)
        field = decode(extended, along_z, along_y, along_x)
        volume = slopes * jnp.sum(slopes * field, axis=0)[None]
        return fold_rims(encode(volume, along_z, along_y, along_x)) + damping_weight * control

    rhs = -fold_rims(encode(slopes * mismatch[None], along_z, along_y, along_x))
    update = jnp.zeros_like(rhs)
    residual = rhs
    image = operate(residual)
    norm_now, product = two_products(residual, image)
    alpha = norm_now / product
    direction, along = (residual, image)
    for step_index in range(ITERS):
        update = update + alpha * direction
        residual = residual - alpha * along
        if step_index + 1 < ITERS:
            image = operate(residual)
            norm_next, product = two_products(residual, image)
            ratio = norm_next / norm_now
            alpha = norm_next / (product - ratio * norm_next / alpha)
            direction = residual + ratio * direction
            along = image + ratio * along
            norm_now = norm_next
    return (update, residual)


def solution(mesh):
    return jax.shard_map(
        shards,
        mesh=mesh,
        in_specs=(P("gz", "gy", None), P("gz", "gy", None)),
        out_specs=(P(None, "gz", "gy", None), P(None, "gz", "gy", None)),
        check_vma=False,
    )
```

profile of v0, /device:TPU:0, one launch (start us, length us, event | category | flops | bytes accessed | tf_op | source)
XLA Modules:
  0.0 264.6 jit_solution(10514513862206553743)
XLA Ops:
  0.6 4.7 %copy_bitcast_fusion = (f32[1,32,64,256]{3,1,2,0:T(8,128)S(1)}, f32[1,32,64,256]{3,1,2,0:T(8,128)S(1)}) fusion(f32[32,64,256]{2,1,0:T(8,128)} %param.27, f32[32,64,256]{2,1,0:T(8,128)} %param.26), kind=kLoop, calls=%fused_computation.51 | loop fusion | bytes 8388608 | tf_op jit(solution)/shard_map/stack | solution.py:95
  5.5 4.9 %collective-permute-start = (f32[2,3,64,256]{3,1,2,0:T(4,128)S(1)}, f32[2,3,64,256]{3,1,2,0:T(4,128)S(1)}, u32[]{:S(2)}, u32[]{:S(2)}) collective-permute-start(f32[2,3,64,256]{3,1,2,0:T(4,128)S(1)} %get-tuple-element.156), channel_id=1, source_target_pairs={{0,8},{8,16},{16,24},{1,9},{9,17},{17,25},{2,10},{10,18},{18,26},{... | collective-permute-start | bytes 1179656 | tf_op jit(solution)/shard_map/ppermute | solution.py:25
  10.4 1.3 collective-permute-start.1
  11.8 9.7 %collective-permute-done = f32[2,3,64,256]{3,1,2,0:T(4,128)S(1)} collective-permute-done((f32[2,3,64,256]{3,1,2,0:T(4,128)S(1)}, f32[2,3,64,256]{3,1,2,0:T(4,128)S(1)}, u32[]{:S(2)}, u32[]{:S(2)}) %collective-permute-start) | collective-permute-done | bytes 393248 | tf_op jit(solution)/shard_map/ppermute | solution.py:25
  21.5 13.2 %collective-permute-done.1 = f32[2,3,64,256]{3,1,2,0:T(4,128)S(1)} collective-permute-done((f32[2,3,64,256]{3,1,2,0:T(4,128)S(1)}, f32[2,3,64,256]{3,1,2,0:T(4,128)S(1)}, u32[]{:S(2)}, u32[]{:S(2)}) %collective-permute-start.1) | collective-permute-done | bytes 393248 | tf_op jit(solution)/shard_map/ppermute | solution.py:27
  34.8 1.3 collective-permute-start.2
  36.1 1.8 collective-permute-start.3
  37.9 0.4 sub.214
  38.2 2.6 copy.6
  40.8 0.5 collective-permute-done.3
  41.3 1.0 pad_maximum_fusion
  42.3 0.4 fusion.9
  42.7 8.0 %fusion.51 = (bf16[1,32,64,256]{3,1,2,0:T(8,128)(2,1)}, bf16[1,32,64,256]{3,1,2,0:T(8,128)(2,1)}, bf16[1,32,64,256]{3,1,2,0:T(8,128)(2,1)}) fusion(f32[38,70,256]{2,0,1:T(8,128)S(1)} %fusion.9), kind=kLoop, calls=%fused_computation.69 | loop fusion | flops 14155776 | bytes 31178752 | tf_op jit(solution)/shard_map/stack | solution.py:99
  50.7 6.4 %fusion.41 = f32[3,8,64,256]{3,1,2,0:T(8,128)S(1)} fusion(f32[32,64,256]{2,0,1:T(8,128)} %copy.6, f32[32]{0:T(128)S(1)} %get-tuple-element.198, s32[32]{0:T(128)S(1)} %get-tuple-element.203, f32[32]{0:T(128)S(1)} %get-tuple-element.190, s32[32]{0:T(128)S(1)} %get-tuple-element.205, f32[32]{0:T(128)S(1)} %get-tuple-element.197, ...), kind=kOutput, calls=%fused_computation.63 | convolution fusion | flops 157289216 | bytes 6816768 | tf_op jit(solution)/shard_map/za,czyx->cayx/dot_general | solution.py:62
  57.1 1.3 fusion.42
  58.5 0.5 fusion.86
  58.9 1.4 collective-permute-start.4
  60.4 4.5 %collective-permute-start.5 = (f32[3,2,12,32]{3,2,1,0:T(8,128)S(1)}, f32[3,2,12,32]{3,2,1,0:T(8,128)S(1)}, u32[]{:S(2)}, u32[]{:S(2)}) collective-permute-start(f32[3,2,12,32]{3,2,1,0:T(8,128)S(1)} %get-tuple-element.165), channel_id=1, source_target_pairs={{0,8},{8,16},{16,24},{1,9},{9,17},{17,25},{2,10},{10,18},{18,26},{... | collective-permute-start | bytes 27656 | tf_op jit(solution)/shard_map/ppermute | solution.py:14
  65.1 1.6 collective-permute-done.5
  66.7 1.3 collective-permute-start.6
  68.0 6.2 %collective-permute-start.7 = (f32[3,4,2,32]{3,2,1,0:T(2,128)S(1)}, f32[3,4,2,32]{3,2,1,0:T(2,128)S(1)}, u32[]{:S(2)}, u32[]{:S(2)}) collective-permute-start(f32[3,4,2,32]{3,2,1,0:T(2,128)S(1)} %get-tuple-element.177), channel_id=1, source_target_pairs={{0,1},{1,2},{2,3},{3,4},{4,5},{5,6},{6,7},{8,9},{9,10},{10,11},{11... | collective-permute-start | bytes 9224 | tf_op jit(solution)/shard_map/ppermute | solution.py:14
  74.3 0.6 collective-permute-done.7
  74.9 4.3 %collective-permute-start.8 = (f32[3,2,8,32]{3,2,1,0:T(8,128)S(1)}, f32[3,2,8,32]{3,2,1,0:T(8,128)S(1)}, u32[]{:S(2)}, u32[]{:S(2)}) collective-permute-start(f32[3,2,8,32]{3,2,1,0:T(8,128)S(1)} %get-tuple-element.181), channel_id=1, source_target_pairs={{0,8},{8,16},{16,24},{1,9},{9,17},{17,25},{2,10},{10,18},{18,26},{... | collective-permute-start | bytes 18440 | tf_op jit(solution)/shard_map/ppermute | solution.py:25
  79.2 1.3 collective-permute-start.9
  80.5 0.2 collective-permute-done.8
  80.7 5.1 %collective-permute-done.9 = f32[3,2,8,32]{3,2,1,0:T(8,128)S(1)} collective-permute-done((f32[3,2,8,32]{3,2,1,0:T(8,128)S(1)}, f32[3,2,8,32]{3,2,1,0:T(8,128)S(1)}, u32[]{:S(2)}, u32[]{:S(2)}) %collective-permute-start.9) | collective-permute-done | bytes 6176 | tf_op jit(solution)/shard_map/ppermute | solution.py:27
  85.9 2.5 collective-permute-start.10
  88.4 1.3 collective-permute-start.11
  89.7 4.7 %collective-permute-done.11 = f32[3,8,2,32]{3,2,1,0:T(2,128)S(1)} collective-permute-done((f32[3,8,2,32]{3,2,1,0:T(2,128)S(1)}, f32[3,8,2,32]{3,2,1,0:T(2,128)S(1)}, u32[]{:S(2)}, u32[]{:S(2)}) %collective-permute-start.11) | collective-permute-done | bytes 6176 | tf_op jit(solution)/shard_map/ppermute | solution.py:27
  94.4 0.5 fusion.54
  94.9 1.4 convolution_bitcast_fusion.1
  96.4 6.1 %fusion.1 = f32[32,64,256]{2,0,1:T(8,128)S(1)} fusion(f32[3,8,64,256]{3,2,1,0:T(8,128)S(1)} %convolution_bitcast_fusion.1, f32[32]{0:T(128)S(1)} %get-tuple-element.198, s32[32]{0:T(128)S(1)} %get-tuple-element.203, f32[32]{0:T(128)S(1)} %get-tuple-element.190, s32[32]{0:T(128)S(1)} %get-tuple-element.205, f32[32]{0:T(128)S(1)} %get-tuple-element.197, ...), kind=kOutput, calls=%fused_computation.12 | convolution fusion | flops 158337792 | bytes 6816768 | tf_op jit(solution)/shard_map/za,cayx->czyx/dot_general | solution.py:57
  102.5 4.1 %fusion.40 = f32[3,8,64,256]{3,1,2,0:T(8,128)S(1)} fusion(f32[32,64,256]{2,0,1:T(8,128)S(1)} %fusion.1, f32[32]{0:T(128)S(1)} %get-tuple-element.198, s32[32]{0:T(128)S(1)} %get-tuple-element.203, f32[32]{0:T(128)S(1)} %get-tuple-element.190, s32[32]{0:T(128)S(1)} %get-tuple-element.205, f32[32]{0:T(128)S(1)} %get-tuple-element.197, ...), kind=kOutput, calls=%fused_computation.62 | convolution fusion | flops 157289216 | bytes 6816768 | tf_op jit(solution)/shard_map/za,czyx->cayx/dot_general | solution.py:62
  106.5 1.3 fusion.45
  107.9 0.5 fusion.83
  108.4 1.3 collective-permute-start.12
  109.7 5.4 %collective-permute-start.13 = (f32[3,2,12,32]{3,2,1,0:T(8,128)S(1)}, f32[3,2,12,32]{3,2,1,0:T(8,128)S(1)}, u32[]{:S(2)}, u32[]{:S(2)}) collective-permute-start(f32[3,2,12,32]{3,2,1,0:T(8,128)S(1)} %get-tuple-element.163), channel_id=1, source_target_pairs={{0,8},{8,16},{16,24},{1,9},{9,17},{17,25},{2,10},{10,18},{18,26},{... | collective-permute-start | bytes 27656 | tf_op jit(solution)/shard_map/ppermute | solution.py:14
  115.3 1.6 collective-permute-done.13
  116.9 1.3 collective-permute-start.14
  118.2 4.2 %collective-permute-start.15 = (f32[3,4,2,32]{3,2,1,0:T(2,128)S(1)}, f32[3,4,2,32]{3,2,1,0:T(2,128)S(1)}, u32[]{:S(2)}, u32[]{:S(2)}) collective-permute-start(f32[3,4,2,32]{3,2,1,0:T(2,128)S(1)} %get-tuple-element.173), channel_id=1, source_target_pairs={{0,1},{1,2},{2,3},{3,4},{4,5},{5,6},{6,7},{8,9},{9,10},{10,11},{11... | collective-permute-start | bytes 9224 | tf_op jit(solution)/shard_map/ppermute | solution.py:14
  122.5 0.8 collective-permute-done.15
  123.3 0.6 multiply_reduce_fusion.2
  123.9 44.3 %all-reduce.2 = (f32[]{:T(128)}, f32[]{:T(128)}) all-reduce(f32[]{:T(128)} %get-tuple-element.149, f32[]{:T(128)} %get-tuple-element.148), channel_id=1, replica_groups=mesh['gz'=4,'gy'=8] {'gz','gy'}, use_global_device_ids=true, to_apply=%region_1.2 | all-reduce | flops 2 | bytes 16 | tf_op jit(solution)/shard_map/psum | solution.py:90
  169.6 4.2 %collective-permute-start.16 = (f32[3,2,8,32]{3,2,1,0:T(8,128)S(1)}, f32[3,2,8,32]{3,2,1,0:T(8,128)S(1)}, u32[]{:S(2)}, u32[]{:S(2)}) collective-permute-start(f32[3,2,8,32]{3,2,1,0:T(8,128)S(1)} %get-tuple-element.179), channel_id=1, source_target_pairs={{0,8},{8,16},{16,24},{1,9},{9,17},{17,25},{2,10},{10,18},{18,26},{... | collective-permute-start | bytes 18440 | tf_op jit(solution)/shard_map/ppermute | solution.py:25
  173.8 1.3 collective-permute-start.17
  175.3 4.2 %collective-permute-done.17 = f32[3,2,8,32]{3,2,1,0:T(8,128)S(1)} collective-permute-done((f32[3,2,8,32]{3,2,1,0:T(8,128)S(1)}, f32[3,2,8,32]{3,2,1,0:T(8,128)S(1)}, u32[]{:S(2)}, u32[]{:S(2)}) %collective-permute-start.17) | collective-permute-done | bytes 6176 | tf_op jit(solution)/shard_map/ppermute | solution.py:27
  179.6 1.5 collective-permute-start.18
  181.1 1.3 collective-permute-start.19
  182.4 3.5 %collective-permute-done.19 = f32[3,8,2,32]{3,2,1,0:T(2,128)S(1)} collective-permute-done((f32[3,8,2,32]{3,2,1,0:T(2,128)S(1)}, f32[3,8,2,32]{3,2,1,0:T(2,128)S(1)}, u32[]{:S(2)}, u32[]{:S(2)}) %collective-permute-start.19) | collective-permute-done | bytes 6176 | tf_op jit(solution)/shard_map/ppermute | solution.py:27
  185.9 0.5 fusion.64
  186.3 1.4 convolution_bitcast_fusion
  187.8 6.1 %fusion.3 = f32[32,64,256]{2,0,1:T(8,128)S(1)} fusion(f32[3,8,64,256]{3,2,1,0:T(8,128)S(1)} %convolution_bitcast_fusion, f32[32]{0:T(128)S(1)} %get-tuple-element.198, s32[32]{0:T(128)S(1)} %get-tuple-element.203, f32[32]{0:T(128)S(1)} %get-tuple-element.190, s32[32]{0:T(128)S(1)} %get-tuple-element.205, f32[32]{0:T(128)S(1)} %get-tuple-element.197, ...), kind=kOutput, calls=%fused_computation.14 | convolution fusion | flops 158337792 | bytes 6816768 | tf_op jit(solution)/shard_map/za,cayx->czyx/dot_general | solution.py:57
  193.9 4.1 %fusion.39 = f32[3,8,64,256]{3,1,2,0:T(8,128)S(1)} fusion(f32[32,64,256]{2,0,1:T(8,128)S(1)} %fusion.3, f32[32]{0:T(128)S(1)} %get-tuple-element.198, s32[32]{0:T(128)S(1)} %get-tuple-element.203, f32[32]{0:T(128)S(1)} %get-tuple-element.190, s32[32]{0:T(128)S(1)} %get-tuple-element.205, f32[32]{0:T(128)S(1)} %get-tuple-element.197, ...), kind=kOutput, calls=%fused_computation.61 | convolution fusion | flops 157289216 | bytes 6816768 | tf_op jit(solution)/shard_map/za,czyx->cayx/dot_general | solution.py:62
  198.0 1.3 fusion.48
  199.3 0.5 fusion.80
  199.8 1.3 collective-permute-start.20
  201.1 5.1 %collective-permute-start.21 = (f32[3,2,12,32]{3,2,1,0:T(8,128)S(1)}, f32[3,2,12,32]{3,2,1,0:T(8,128)S(1)}, u32[]{:S(2)}, u32[]{:S(2)}) collective-permute-start(f32[3,2,12,32]{3,2,1,0:T(8,128)S(1)} %get-tuple-element.161), channel_id=1, source_target_pairs={{0,8},{8,16},{16,24},{1,9},{9,17},{17,25},{2,10},{10,18},{18,26},{... | collective-permute-start | bytes 27656 | tf_op jit(solution)/shard_map/ppermute | solution.py:14
  206.4 1.6 collective-permute-done.21
  208.0 1.3 collective-permute-start.22
  209.3 4.2 %collective-permute-start.23 = (f32[3,4,2,32]{3,2,1,0:T(2,128)S(1)}, f32[3,4,2,32]{3,2,1,0:T(2,128)S(1)}, u32[]{:S(2)}, u32[]{:S(2)}) collective-permute-start(f32[3,4,2,32]{3,2,1,0:T(2,128)S(1)} %get-tuple-element.169), channel_id=1, source_target_pairs={{0,1},{1,2},{2,3},{3,4},{4,5},{5,6},{6,7},{8,9},{9,10},{10,11},{11... | collective-permute-start | bytes 9224 | tf_op jit(solution)/shard_map/ppermute | solution.py:14
  213.6 0.8 collective-permute-done.23
  214.4 0.7 multiply_reduce_fusion
  215.1 44.3 %all-reduce.1 = (f32[]{:T(128)}, f32[]{:T(128)}) all-reduce(f32[]{:T(128)} %get-tuple-element.147, f32[]{:T(128)} %get-tuple-element.146), channel_id=1, replica_groups=mesh['gz'=4,'gy'=8] {'gz','gy'}, use_global_device_ids=true, to_apply=%region_6.7 | all-reduce | flops 2 | bytes 16 | tf_op jit(solution)/shard_map/psum | solution.py:90
  263.7 0.7 multiply_subtract_fusion
  (64 shorter events, 1.3 us)
Async XLA Ops:
  5.5 16.0 %collective-permute-start = (f32[2,3,64,256]{3,1,2,0:T(4,128)S(1)}, f32[2,3,64,256]{3,1,2,0:T(4,128)S(1)}, u32[]{:S(2)}, u32[]{:S(2)}) collective-permute-start(f32[2,3,64,256]{3,1,2,0:T(4,128)S(1)} %get-tuple-element.156), channel_id=1, source_target_pairs={{0,8},{8,16},{16,24},{1,9},{9,17},{17,25},{2,10},{10,18},{18,26},{... | collective-permute-start | bytes 1179656 | tf_op jit(solution)/shard_map/ppermute | solution.py:25
  10.4 24.3 %collective-permute-start.1 = (f32[2,3,64,256]{3,1,2,0:T(4,128)S(1)}, f32[2,3,64,256]{3,1,2,0:T(4,128)S(1)}, u32[]{:S(2)}, u32[]{:S(2)}) collective-permute-start(f32[2,3,64,256]{3,1,2,0:T(4,128)S(1)} %get-tuple-element.157), channel_id=1, source_target_pairs={{8,0},{16,8},{24,16},{9,1},{17,9},{25,17},{10,2},{18,10},{26,18},{... | collective-permute-start | bytes 1179656 | tf_op jit(solution)/shard_map/ppermute | solution.py:27
  11.8 26.1 %copy-start.3 = (f32[32,64,256]{2,1,0:T(8,128)S(1)}, f32[32,64,256]{2,1,0:T(8,128)}, u32[]{:S(2)}) copy-start(f32[32,64,256]{2,1,0:T(8,128)} %param.27) | copy-start | bytes 6291460
  11.8 26.0 %copy-start.4 = (f32[32,64,256]{2,1,0:T(8,128)S(1)}, f32[32,64,256]{2,1,0:T(8,128)}, u32[]{:S(2)}) copy-start(f32[32,64,256]{2,1,0:T(8,128)} %param.26) | copy-start | bytes 6291460
  34.8 6.1 %collective-permute-start.2 = (f32[2,38,3,256]{3,1,2,0:T(8,128)S(1)}, f32[2,38,3,256]{3,1,2,0:T(8,128)S(1)}, u32[]{:S(2)}, u32[]{:S(2)}) collective-permute-start(f32[2,38,3,256]{3,1,2,0:T(8,128)S(1)} %get-tuple-element.154), channel_id=1, source_target_pairs={{0,1},{1,2},{2,3},{3,4},{4,5},{5,6},{6,7},{8,9},{9,10},{10,11},{11... | collective-permute-start | bytes 700424 | tf_op jit(solution)/shard_map/ppermute | solution.py:25
  36.1 5.2 %collective-permute-start.3 = (f32[2,38,3,256]{3,1,2,0:T(8,128)S(1)}, f32[2,38,3,256]{3,1,2,0:T(8,128)S(1)}, u32[]{:S(2)}, u32[]{:S(2)}) collective-permute-start(f32[2,38,3,256]{3,1,2,0:T(8,128)S(1)} %get-tuple-element.155), channel_id=1, source_target_pairs={{1,0},{2,1},{3,2},{4,3},{5,4},{6,5},{7,6},{9,8},{10,9},{11,10},{12... | collective-permute-start | bytes 700424 | tf_op jit(solution)/shard_map/ppermute | solution.py:27
  58.4 37.9 %copy-start = (bf16[1,32,64,256]{3,1,2,0:T(8,128)(2,1)S(1)}, bf16[1,32,64,256]{3,1,2,0:T(8,128)(2,1)}, u32[]{:S(2)}) copy-start(bf16[1,32,64,256]{3,1,2,0:T(8,128)(2,1)} %get-tuple-element.158) | copy-start | bytes 3145732
  58.4 37.9 %copy-start.1 = (bf16[1,32,64,256]{3,1,2,0:T(8,128)(2,1)S(1)}, bf16[1,32,64,256]{3,1,2,0:T(8,128)(2,1)}, u32[]{:S(2)}) copy-start(bf16[1,32,64,256]{3,1,2,0:T(8,128)(2,1)} %get-tuple-element.159) | copy-start | bytes 3145732
  58.4 37.9 %copy-start.2 = (bf16[1,32,64,256]{3,1,2,0:T(8,128)(2,1)S(1)}, bf16[1,32,64,256]{3,1,2,0:T(8,128)(2,1)}, u32[]{:S(2)}) copy-start(bf16[1,32,64,256]{3,1,2,0:T(8,128)(2,1)} %get-tuple-element.160) | copy-start | bytes 3145732
  58.9 6.1 %collective-permute-start.4 = (f32[3,2,12,32]{3,2,1,0:T(8,128)S(1)}, f32[3,2,12,32]{3,2,1,0:T(8,128)S(1)}, u32[]{:S(2)}, u32[]{:S(2)}) collective-permute-start(f32[3,2,12,32]{3,2,1,0:T(8,128)S(1)} %get-tuple-element.166), channel_id=1, source_target_pairs={{8,0},{16,8},{24,16},{9,1},{17,9},{25,17},{10,2},{18,10},{26,18},{... | collective-permute-start | bytes 27656 | tf_op jit(solution)/shard_map/ppermute | solution.py:14
  60.4 6.3 %collective-permute-start.5 = (f32[3,2,12,32]{3,2,1,0:T(8,128)S(1)}, f32[3,2,12,32]{3,2,1,0:T(8,128)S(1)}, u32[]{:S(2)}, u32[]{:S(2)}) collective-permute-start(f32[3,2,12,32]{3,2,1,0:T(8,128)S(1)} %get-tuple-element.165), channel_id=1, source_target_pairs={{0,8},{8,16},{16,24},{1,9},{9,17},{17,25},{2,10},{10,18},{18,26},{... | collective-permute-start | bytes 27656 | tf_op jit(solution)/shard_map/ppermute | solution.py:14
  66.7 7.5 %collective-permute-start.6 = (f32[3,4,2,32]{3,2,1,0:T(2,128)S(1)}, f32[3,4,2,32]{3,2,1,0:T(2,128)S(1)}, u32[]{:S(2)}, u32[]{:S(2)}) collective-permute-start(f32[3,4,2,32]{3,2,1,0:T(2,128)S(1)} %get-tuple-element.178), channel_id=1, source_target_pairs={{1,0},{2,1},{3,2},{4,3},{5,4},{6,5},{7,6},{9,8},{10,9},{11,10},{12... | collective-permute-start | bytes 9224 | tf_op jit(solution)/shard_map/ppermute | solution.py:14
  68.0 6.8 %collective-permute-start.7 = (f32[3,4,2,32]{3,2,1,0:T(2,128)S(1)}, f32[3,4,2,32]{3,2,1,0:T(2,128)S(1)}, u32[]{:S(2)}, u32[]{:S(2)}) collective-permute-start(f32[3,4,2,32]{3,2,1,0:T(2,128)S(1)} %get-tuple-element.177), channel_id=1, source_target_pairs={{0,1},{1,2},{2,3},{3,4},{4,5},{5,6},{6,7},{8,9},{9,10},{10,11},{11... | collective-permute-start | bytes 9224 | tf_op jit(solution)/shard_map/ppermute | solution.py:14
  74.9 5.8 %collective-permute-start.8 = (f32[3,2,8,32]{3,2,1,0:T(8,128)S(1)}, f32[3,2,8,32]{3,2,1,0:T(8,128)S(1)}, u32[]{:S(2)}, u32[]{:S(2)}) collective-permute-start(f32[3,2,8,32]{3,2,1,0:T(8,128)S(1)} %get-tuple-element.181), channel_id=1, source_target_pairs={{0,8},{8,16},{16,24},{1,9},{9,17},{17,25},{2,10},{10,18},{18,26},{... | collective-permute-start | bytes 18440 | tf_op jit(solution)/shard_map/ppermute | solution.py:25
  79.2 6.7 %collective-permute-start.9 = (f32[3,2,8,32]{3,2,1,0:T(8,128)S(1)}, f32[3,2,8,32]{3,2,1,0:T(8,128)S(1)}, u32[]{:S(2)}, u32[]{:S(2)}) collective-permute-start(f32[3,2,8,32]{3,2,1,0:T(8,128)S(1)} %get-tuple-element.182), channel_id=1, source_target_pairs={{8,0},{16,8},{24,16},{9,1},{17,9},{25,17},{10,2},{18,10},{26,18},{... | collective-permute-start | bytes 18440 | tf_op jit(solution)/shard_map/ppermute | solution.py:27
  85.9 3.8 %collective-permute-start.10 = (f32[3,8,2,32]{3,2,1,0:T(2,128)S(1)}, f32[3,8,2,32]{3,2,1,0:T(2,128)S(1)}, u32[]{:S(2)}, u32[]{:S(2)}) collective-permute-start(f32[3,8,2,32]{3,2,1,0:T(2,128)S(1)} %get-tuple-element.175), channel_id=1, source_target_pairs={{0,1},{1,2},{2,3},{3,4},{4,5},{5,6},{6,7},{8,9},{9,10},{10,11},{11... | collective-permute-start | bytes 18440 | tf_op jit(solution)/shard_map/ppermute | solution.py:25
  88.4 6.0 %collective-permute-start.11 = (f32[3,8,2,32]{3,2,1,0:T(2,128)S(1)}, f32[3,8,2,32]{3,2,1,0:T(2,128)S(1)}, u32[]{:S(2)}, u32[]{:S(2)}) collective-permute-start(f32[3,8,2,32]{3,2,1,0:T(2,128)S(1)} %get-tuple-element.176), channel_id=1, source_target_pairs={{1,0},{2,1},{3,2},{4,3},{5,4},{6,5},{7,6},{9,8},{10,9},{11,10},{12... | collective-permute-start | bytes 18440 | tf_op jit(solution)/shard_map/ppermute | solution.py:27
  108.4 6.9 %collective-permute-start.12 = (f32[3,2,12,32]{3,2,1,0:T(8,128)S(1)}, f32[3,2,12,32]{3,2,1,0:T(8,128)S(1)}, u32[]{:S(2)}, u32[]{:S(2)}) collective-permute-start(f32[3,2,12,32]{3,2,1,0:T(8,128)S(1)} %get-tuple-element.164), channel_id=1, source_target_pairs={{8,0},{16,8},{24,16},{9,1},{17,9},{25,17},{10,2},{18,10},{26,18},{... | collective-permute-start | bytes 27656 | tf_op jit(solution)/shard_map/ppermute | solution.py:14
  109.7 7.2 %collective-permute-start.13 = (f32[3,2,12,32]{3,2,1,0:T(8,128)S(1)}, f32[3,2,12,32]{3,2,1,0:T(8,128)S(1)}, u32[]{:S(2)}, u32[]{:S(2)}) collective-permute-start(f32[3,2,12,32]{3,2,1,0:T(8,128)S(1)} %get-tuple-element.163), channel_id=1, source_target_pairs={{0,8},{8,16},{16,24},{1,9},{9,17},{17,25},{2,10},{10,18},{18,26},{... | collective-permute-start | bytes 27656 | tf_op jit(solution)/shard_map/ppermute | solution.py:14
  116.9 5.6 %collective-permute-start.14 = (f32[3,4,2,32]{3,2,1,0:T(2,128)S(1)}, f32[3,4,2,32]{3,2,1,0:T(2,128)S(1)}, u32[]{:S(2)}, u32[]{:S(2)}) collective-permute-start(f32[3,4,2,32]{3,2,1,0:T(2,128)S(1)} %get-tuple-element.174), channel_id=1, source_target_pairs={{1,0},{2,1},{3,2},{4,3},{5,4},{6,5},{7,6},{9,8},{10,9},{11,10},{12... | collective-permute-start | bytes 9224 | tf_op jit(solution)/shard_map/ppermute | solution.py:14
  118.2 5.1 %collective-permute-start.15 = (f32[3,4,2,32]{3,2,1,0:T(2,128)S(1)}, f32[3,4,2,32]{3,2,1,0:T(2,128)S(1)}, u32[]{:S(2)}, u32[]{:S(2)}) collective-permute-start(f32[3,4,2,32]{3,2,1,0:T(2,128)S(1)} %get-tuple-element.173), channel_id=1, source_target_pairs={{0,1},{1,2},{2,3},{3,4},{4,5},{5,6},{6,7},{8,9},{9,10},{10,11},{11... | collective-permute-start | bytes 9224 | tf_op jit(solution)/shard_map/ppermute | solution.py:14
  169.6 5.7 %collective-permute-start.16 = (f32[3,2,8,32]{3,2,1,0:T(8,128)S(1)}, f32[3,2,8,32]{3,2,1,0:T(8,128)S(1)}, u32[]{:S(2)}, u32[]{:S(2)}) collective-permute-start(f32[3,2,8,32]{3,2,1,0:T(8,128)S(1)} %get-tuple-element.179), channel_id=1, source_target_pairs={{0,8},{8,16},{16,24},{1,9},{9,17},{17,25},{2,10},{10,18},{18,26},{... | collective-permute-start | bytes 18440 | tf_op jit(solution)/shard_map/ppermute | solution.py:25
  173.8 5.7 %collective-permute-start.17 = (f32[3,2,8,32]{3,2,1,0:T(8,128)S(1)}, f32[3,2,8,32]{3,2,1,0:T(8,128)S(1)}, u32[]{:S(2)}, u32[]{:S(2)}) collective-permute-start(f32[3,2,8,32]{3,2,1,0:T(8,128)S(1)} %get-tuple-element.180), channel_id=1, source_target_pairs={{8,0},{16,8},{24,16},{9,1},{17,9},{25,17},{10,2},{18,10},{26,18},{... | collective-permute-start | bytes 18440 | tf_op jit(solution)/shard_map/ppermute | solution.py:27
  179.6 2.8 %collective-permute-start.18 = (f32[3,8,2,32]{3,2,1,0:T(2,128)S(1)}, f32[3,8,2,32]{3,2,1,0:T(2,128)S(1)}, u32[]{:S(2)}, u32[]{:S(2)}) collective-permute-start(f32[3,8,2,32]{3,2,1,0:T(2,128)S(1)} %get-tuple-element.171), channel_id=1, source_target_pairs={{0,1},{1,2},{2,3},{3,4},{4,5},{5,6},{6,7},{8,9},{9,10},{10,11},{11... | collective-permute-start | bytes 18440 | tf_op jit(solution)/shard_map/ppermute | solution.py:25
  181.1 4.8 %collective-permute-start.19 = (f32[3,8,2,32]{3,2,1,0:T(2,128)S(1)}, f32[3,8,2,32]{3,2,1,0:T(2,128)S(1)}, u32[]{:S(2)}, u32[]{:S(2)}) collective-permute-start(f32[3,8,2,32]{3,2,1,0:T(2,128)S(1)} %get-tuple-element.172), channel_id=1, source_target_pairs={{1,0},{2,1},{3,2},{4,3},{5,4},{6,5},{7,6},{9,8},{10,9},{11,10},{12... | collective-permute-start | bytes 18440 | tf_op jit(solution)/shard_map/ppermute | solution.py:27
  199.8 6.5 %collective-permute-start.20 = (f32[3,2,12,32]{3,2,1,0:T(8,128)S(1)}, f32[3,2,12,32]{3,2,1,0:T(8,128)S(1)}, u32[]{:S(2)}, u32[]{:S(2)}) collective-permute-start(f32[3,2,12,32]{3,2,1,0:T(8,128)S(1)} %get-tuple-element.162), channel_id=1, source_target_pairs={{8,0},{16,8},{24,16},{9,1},{17,9},{25,17},{10,2},{18,10},{26,18},{... | collective-permute-start | bytes 27656 | tf_op jit(solution)/shard_map/ppermute | solution.py:14
  201.1 6.8 %collective-permute-start.21 = (f32[3,2,12,32]{3,2,1,0:T(8,128)S(1)}, f32[3,2,12,32]{3,2,1,0:T(8,128)S(1)}, u32[]{:S(2)}, u32[]{:S(2)}) collective-permute-start(f32[3,2,12,32]{3,2,1,0:T(8,128)S(1)} %get-tuple-element.161), channel_id=1, source_target_pairs={{0,8},{8,16},{16,24},{1,9},{9,17},{17,25},{2,10},{10,18},{18,26},{... | collective-permute-start | bytes 27656 | tf_op jit(solution)/shard_map/ppermute | solution.py:14
  208.0 5.6 %collective-permute-start.22 = (f32[3,4,2,32]{3,2,1,0:T(2,128)S(1)}, f32[3,4,2,32]{3,2,1,0:T(2,128)S(1)}, u32[]{:S(2)}, u32[]{:S(2)}) collective-permute-start(f32[3,4,2,32]{3,2,1,0:T(2,128)S(1)} %get-tuple-element.170), channel_id=1, source_target_pairs={{1,0},{2,1},{3,2},{4,3},{5,4},{6,5},{7,6},{9,8},{10,9},{11,10},{12... | collective-permute-start | bytes 9224 | tf_op jit(solution)/shard_map/ppermute | solution.py:14
  209.3 5.1 %collective-permute-start.23 = (f32[3,4,2,32]{3,2,1,0:T(2,128)S(1)}, f32[3,4,2,32]{3,2,1,0:T(2,128)S(1)}, u32[]{:S(2)}, u32[]{:S(2)}) collective-permute-start(f32[3,4,2,32]{3,2,1,0:T(2,128)S(1)} %get-tuple-element.169), channel_id=1, source_target_pairs={{0,1},{1,2},{2,3},{3,4},{4,5},{5,6},{6,7},{8,9},{9,10},{10,11},{11... | collective-permute-start | bytes 9224 | tf_op jit(solution)/shard_map/ppermute | solution.py:14
where the time goes:
time: 269 us; the launch traced here: 265 us
  blocking collectives  88.6 us (33%)
  starting transfers between devices  64.5 us (24%)
  waiting for transfers between devices  48.6 us (18%)
  matrix products  35.9 us (13%)
  other arithmetic  12.3 us (5%)
  local copies, waits for them, and re-layouts  7.36 us (3%)
  between operations  7.22 us (3%)
    psum x2, blocking collectives, two_products(): lax.psum((jnp.sum(residual * residual), jnp.sum(residual * image)), ('gz'...  88.6 us
    ppermute x12, starting transfers between devices, from_behind(): lax.ppermute(value, axis, [(source, source + steps) for source in range(i...  37.6 us
    ppermute x6, waiting for transfers between devices, padded_2(): lax.ppermute(head, axis, [((i + 1) % count, i) for i in range(ends)])  31.2 us
    ppermute x6, starting transfers between devices, padded_2(): lax.ppermute(tail, axis, [(i, (i + 1) % count) for i in range(ends)])  18.7 us
    dot_general x3, matrix products, encode(): inner = jnp.einsum('za,czyx->cayx', along_z, volume, precision=hp)  14.5 us
    dot_general x2, matrix products, decode(): return jnp.einsum('za,cayx->czyx', along_z, inner, precision=hp)  12.2 us
    ppermute x6, waiting for transfers between devices, padded_2(): lax.ppermute(tail, axis, [(i, (i + 1) % count) for i in range(ends)])  10.1 us
    ppermute x6, starting transfers between devices, padded_2(): lax.ppermute(head, axis, [((i + 1) % count, i) for i in range(ends)])  8.22 us
  transfers between devices with their start and end apart: 24, of which 18 were waited for; matrix products, arithmetic and copies ran while one was open for 1% of the time, Pallas kernels for 0%

commit v1 on v0

--- a/solution.py
+++ b/solution.py
@@ -6,6 +6,11 @@
 SPACING = 8
 ITERS = 2
 damping_weight = 8.0
+
+
+def by_each_axis(array, axis_one, axis_two):
+    half = lax.psum(array, axis_one)
+    return lax.psum(half, axis_two)
 
 
 def from_behind(value, axis, steps):
@@ -87,7 +92,7 @@
 
 
 def two_products(residual, image):
-    return lax.psum((jnp.sum(residual * residual), jnp.sum(residual * image)), ("gz", "gy"))
+    return by_each_axis((jnp.sum(residual * residual), jnp.sum(residual * image)), "gy", "gz")
 
 
 def shards(fixed, moving):

time: 269 us -> 232 us (0.86)
  blocking collectives: 88.6 us -> 55.9 us
    psum x2 -> x4, blocking collectives: 88.6 us -> 55.9 us  [the longest x2 33.7 us: by_each_axis(): half = lax.psum(array, axis_one)]
where the time goes in v1:
time: 232 us; the launch traced here: 228 us
  starting transfers between devices  62.4 us (27%)
  blocking collectives  55.9 us (24%)
  waiting for transfers between devices  46.7 us (20%)
  matrix products  35.9 us (15%)
  other arithmetic  12.3 us (5%)
  local copies, waits for them, and re-layouts  7.38 us (3%)
  between operations  7.28 us (3%)
    ppermute x12, starting transfers between devices, from_behind(): lax.ppermute(value, axis, [(source, source + steps) for source in range(i...  35.9 us
    psum x2, blocking collectives, by_each_axis(): half = lax.psum(array, axis_one)  33.7 us
    ppermute x6, waiting for transfers between devices, padded_2(): lax.ppermute(head, axis, [((i + 1) % count, i) for i in range(ends)])  29.3 us
    psum x2, blocking collectives, by_each_axis(): return lax.psum(half, axis_two)  22.1 us
    ppermute x6, starting transfers between devices, padded_2(): lax.ppermute(tail, axis, [(i, (i + 1) % count) for i in range(ends)])  18.1 us
    dot_general x3, matrix products, encode(): inner = jnp.einsum('za,czyx->cayx', along_z, volume, precision=hp)  14.5 us
    dot_general x2, matrix products, decode(): return jnp.einsum('za,cayx->czyx', along_z, inner, precision=hp)  12.2 us
    ppermute x6, waiting for transfers between devices, padded_2(): lax.ppermute(tail, axis, [(i, (i + 1) % count) for i in range(ends)])  10.1 us
  transfers between devices with their start and end apart: 24, of which 18 were waited for; matrix products, arithmetic and copies ran while one was open for 1% of the time, Pallas kernels for 0%

profile of v1, /device:TPU:0, one launch (start us, length us, event | category | flops | bytes accessed | tf_op | source)
XLA Modules:
  0.0 227.9 jit_solution(4259805977871045244)
XLA Ops:
  0.6 4.7 %copy_bitcast_fusion = (f32[1,32,64,256]{3,1,2,0:T(8,128)S(1)}, f32[1,32,64,256]{3,1,2,0:T(8,128)S(1)}) fusion(f32[32,64,256]{2,1,0:T(8,128)} %param.27, f32[32,64,256]{2,1,0:T(8,128)} %param.26), kind=kLoop, calls=%fused_computation.51 | loop fusion | bytes 8388608 | tf_op jit(solution)/shard_map/stack | solution.py:100
  5.5 4.9 %collective-permute-start = (f32[2,3,64,256]{3,1,2,0:T(4,128)S(1)}, f32[2,3,64,256]{3,1,2,0:T(4,128)S(1)}, u32[]{:S(2)}, u32[]{:S(2)}) collective-permute-start(f32[2,3,64,256]{3,1,2,0:T(4,128)S(1)} %get-tuple-element.160), channel_id=1, source_target_pairs={{0,8},{8,16},{16,24},{1,9},{9,17},{17,25},{2,10},{10,18},{18,26},{... | collective-permute-start | bytes 1179656 | tf_op jit(solution)/shard_map/ppermute | solution.py:30
  10.4 1.3 collective-permute-start.1
  11.8 9.7 %collective-permute-done = f32[2,3,64,256]{3,1,2,0:T(4,128)S(1)} collective-permute-done((f32[2,3,64,256]{3,1,2,0:T(4,128)S(1)}, f32[2,3,64,256]{3,1,2,0:T(4,128)S(1)}, u32[]{:S(2)}, u32[]{:S(2)}) %collective-permute-start) | collective-permute-done | bytes 393248 | tf_op jit(solution)/shard_map/ppermute | solution.py:30
  21.5 13.2 %collective-permute-done.1 = f32[2,3,64,256]{3,1,2,0:T(4,128)S(1)} collective-permute-done((f32[2,3,64,256]{3,1,2,0:T(4,128)S(1)}, f32[2,3,64,256]{3,1,2,0:T(4,128)S(1)}, u32[]{:S(2)}, u32[]{:S(2)}) %collective-permute-start.1) | collective-permute-done | bytes 393248 | tf_op jit(solution)/shard_map/ppermute | solution.py:32
  34.8 1.3 collective-permute-start.2
  36.1 1.8 collective-permute-start.3
  38.2 2.6 %copy.6 = f32[32,64,256]{2,0,1:T(8,128)} copy(f32[32,64,256]{2,1,0:T(8,128)S(1)} %sub.214) | data formatting | bytes 4194304 | tf_op jit(solution)/shard_map/sub | solution.py:111
  40.9 0.4 collective-permute-done.3
  41.3 1.0 pad_maximum_fusion
  42.7 8.0 %fusion.51 = (bf16[1,32,64,256]{3,1,2,0:T(8,128)(2,1)}, bf16[1,32,64,256]{3,1,2,0:T(8,128)(2,1)}, bf16[1,32,64,256]{3,1,2,0:T(8,128)(2,1)}) fusion(f32[38,70,256]{2,0,1:T(8,128)S(1)} %fusion.9), kind=kLoop, calls=%fused_computation.69 | loop fusion | flops 14155776 | bytes 31178752 | tf_op jit(solution)/shard_map/stack | solution.py:104
  50.7 6.4 %fusion.41 = f32[3,8,64,256]{3,1,2,0:T(8,128)S(1)} fusion(f32[32,64,256]{2,0,1:T(8,128)} %copy.6, f32[32]{0:T(128)S(1)} %get-tuple-element.202, s32[32]{0:T(128)S(1)} %get-tuple-element.207, f32[32]{0:T(128)S(1)} %get-tuple-element.194, s32[32]{0:T(128)S(1)} %get-tuple-element.209, f32[32]{0:T(128)S(1)} %get-tuple-element.201, ...), kind=kOutput, calls=%fused_computation.63 | convolution fusion | flops 157289216 | bytes 6816768 | tf_op jit(solution)/shard_map/za,czyx->cayx/dot_general | solution.py:67
  57.1 1.3 fusion.42
  58.5 0.5 fusion.86
  59.0 1.4 collective-permute-start.4
  60.4 4.5 %collective-permute-start.5 = (f32[3,2,12,32]{3,2,1,0:T(8,128)S(1)}, f32[3,2,12,32]{3,2,1,0:T(8,128)S(1)}, u32[]{:S(2)}, u32[]{:S(2)}) collective-permute-start(f32[3,2,12,32]{3,2,1,0:T(8,128)S(1)} %get-tuple-element.169), channel_id=1, source_target_pairs={{0,8},{8,16},{16,24},{1,9},{9,17},{17,25},{2,10},{10,18},{18,26},{... | collective-permute-start | bytes 27656 | tf_op jit(solution)/shard_map/ppermute | solution.py:19
  65.1 1.6 collective-permute-done.5
  66.7 1.3 collective-permute-start.6
  68.1 6.2 %collective-permute-start.7 = (f32[3,4,2,32]{3,2,1,0:T(2,128)S(1)}, f32[3,4,2,32]{3,2,1,0:T(2,128)S(1)}, u32[]{:S(2)}, u32[]{:S(2)}) collective-permute-start(f32[3,4,2,32]{3,2,1,0:T(2,128)S(1)} %get-tuple-element.181), channel_id=1, source_target_pairs={{0,1},{1,2},{2,3},{3,4},{4,5},{5,6},{6,7},{8,9},{9,10},{10,11},{11... | collective-permute-start | bytes 9224 | tf_op jit(solution)/shard_map/ppermute | solution.py:19
  74.3 0.6 collective-permute-done.7
  74.9 4.3 %collective-permute-start.8 = (f32[3,2,8,32]{3,2,1,0:T(8,128)S(1)}, f32[3,2,8,32]{3,2,1,0:T(8,128)S(1)}, u32[]{:S(2)}, u32[]{:S(2)}) collective-permute-start(f32[3,2,8,32]{3,2,1,0:T(8,128)S(1)} %get-tuple-element.185), channel_id=1, source_target_pairs={{0,8},{8,16},{16,24},{1,9},{9,17},{17,25},{2,10},{10,18},{18,26},{... | collective-permute-start | bytes 18440 | tf_op jit(solution)/shard_map/ppermute | solution.py:30
  79.2 1.3 collective-permute-start.9
  80.7 5.1 %collective-permute-done.9 = f32[3,2,8,32]{3,2,1,0:T(8,128)S(1)} collective-permute-done((f32[3,2,8,32]{3,2,1,0:T(8,128)S(1)}, f32[3,2,8,32]{3,2,1,0:T(8,128)S(1)}, u32[]{:S(2)}, u32[]{:S(2)}) %collective-permute-start.9) | collective-permute-done | bytes 6176 | tf_op jit(solution)/shard_map/ppermute | solution.py:32
  85.9 2.5 %collective-permute-start.10 = (f32[3,8,2,32]{3,2,1,0:T(2,128)S(1)}, f32[3,8,2,32]{3,2,1,0:T(2,128)S(1)}, u32[]{:S(2)}, u32[]{:S(2)}) collective-permute-start(f32[3,8,2,32]{3,2,1,0:T(2,128)S(1)} %get-tuple-element.179), channel_id=1, source_target_pairs={{0,1},{1,2},{2,3},{3,4},{4,5},{5,6},{6,7},{8,9},{9,10},{10,11},{11... | collective-permute-start | bytes 18440 | tf_op jit(solution)/shard_map/ppermute | solution.py:30
  88.4 1.3 collective-permute-start.11
  89.7 4.7 %collective-permute-done.11 = f32[3,8,2,32]{3,2,1,0:T(2,128)S(1)} collective-permute-done((f32[3,8,2,32]{3,2,1,0:T(2,128)S(1)}, f32[3,8,2,32]{3,2,1,0:T(2,128)S(1)}, u32[]{:S(2)}, u32[]{:S(2)}) %collective-permute-start.11) | collective-permute-done | bytes 6176 | tf_op jit(solution)/shard_map/ppermute | solution.py:32
  94.4 0.5 fusion.54
  94.9 1.4 convolution_bitcast_fusion.1
  96.4 6.1 %fusion.1 = f32[32,64,256]{2,0,1:T(8,128)S(1)} fusion(f32[3,8,64,256]{3,2,1,0:T(8,128)S(1)} %convolution_bitcast_fusion.1, f32[32]{0:T(128)S(1)} %get-tuple-element.202, s32[32]{0:T(128)S(1)} %get-tuple-element.207, f32[32]{0:T(128)S(1)} %get-tuple-element.194, s32[32]{0:T(128)S(1)} %get-tuple-element.209, f32[32]{0:T(128)S(1)} %get-tuple-element.201, ...), kind=kOutput, calls=%fused_computation.12 | convolution fusion | flops 158337792 | bytes 6816768 | tf_op jit(solution)/shard_map/za,cayx->czyx/dot_general | solution.py:62
  102.5 4.1 %fusion.40 = f32[3,8,64,256]{3,1,2,0:T(8,128)S(1)} fusion(f32[32,64,256]{2,0,1:T(8,128)S(1)} %fusion.1, f32[32]{0:T(128)S(1)} %get-tuple-element.202, s32[32]{0:T(128)S(1)} %get-tuple-element.207, f32[32]{0:T(128)S(1)} %get-tuple-element.194, s32[32]{0:T(128)S(1)} %get-tuple-element.209, f32[32]{0:T(128)S(1)} %get-tuple-element.201, ...), kind=kOutput, calls=%fused_computation.62 | convolution fusion | flops 157289216 | bytes 6816768 | tf_op jit(solution)/shard_map/za,czyx->cayx/dot_general | solution.py:67
  106.6 1.3 fusion.45
  107.9 0.5 fusion.83
  108.4 1.3 collective-permute-start.12
  109.7 5.4 %collective-permute-start.13 = (f32[3,2,12,32]{3,2,1,0:T(8,128)S(1)}, f32[3,2,12,32]{3,2,1,0:T(8,128)S(1)}, u32[]{:S(2)}, u32[]{:S(2)}) collective-permute-start(f32[3,2,12,32]{3,2,1,0:T(8,128)S(1)} %get-tuple-element.167), channel_id=1, source_target_pairs={{0,8},{8,16},{16,24},{1,9},{9,17},{17,25},{2,10},{10,18},{18,26},{... | collective-permute-start | bytes 27656 | tf_op jit(solution)/shard_map/ppermute | solution.py:19
  115.3 1.6 collective-permute-done.13
  116.9 1.3 collective-permute-start.14
  118.3 4.2 %collective-permute-start.15 = (f32[3,4,2,32]{3,2,1,0:T(2,128)S(1)}, f32[3,4,2,32]{3,2,1,0:T(2,128)S(1)}, u32[]{:S(2)}, u32[]{:S(2)}) collective-permute-start(f32[3,4,2,32]{3,2,1,0:T(2,128)S(1)} %get-tuple-element.177), channel_id=1, source_target_pairs={{0,1},{1,2},{2,3},{3,4},{4,5},{5,6},{6,7},{8,9},{9,10},{10,11},{11... | collective-permute-start | bytes 9224 | tf_op jit(solution)/shard_map/ppermute | solution.py:19
  122.5 0.8 collective-permute-done.15
  123.3 0.6 multiply_reduce_fusion.2
  123.9 17.8 %all-reduce.2 = (f32[]{:T(128)}, f32[]{:T(128)}) all-reduce(f32[]{:T(128)} %get-tuple-element.149, f32[]{:T(128)} %get-tuple-element.148), channel_id=1, replica_groups=mesh['gz'=4,'gy'=8] {'gy'}, use_global_device_ids=true, to_apply=%region_1.2 | all-reduce | flops 2 | bytes 16 | tf_op jit(solution)/shard_map/psum | solution.py:12
  141.8 11.0 %all-reduce.4 = (f32[]{:T(128)}, f32[]{:T(128)}) all-reduce(f32[]{:T(128)} %get-tuple-element.152, f32[]{:T(128)} %get-tuple-element.153), channel_id=1, replica_groups=mesh['gz'=4,'gy'=8] {'gz'}, use_global_device_ids=true, to_apply=%region_2.3 | all-reduce | flops 2 | bytes 16 | tf_op jit(solution)/shard_map/psum | solution.py:13
  154.1 3.8 %collective-permute-start.16 = (f32[3,2,8,32]{3,2,1,0:T(8,128)S(1)}, f32[3,2,8,32]{3,2,1,0:T(8,128)S(1)}, u32[]{:S(2)}, u32[]{:S(2)}) collective-permute-start(f32[3,2,8,32]{3,2,1,0:T(8,128)S(1)} %get-tuple-element.183), channel_id=1, source_target_pairs={{0,8},{8,16},{16,24},{1,9},{9,17},{17,25},{2,10},{10,18},{18,26},{... | collective-permute-start | bytes 18440 | tf_op jit(solution)/shard_map/ppermute | solution.py:30
  158.0 1.3 collective-permute-start.17
  159.5 4.2 %collective-permute-done.17 = f32[3,2,8,32]{3,2,1,0:T(8,128)S(1)} collective-permute-done((f32[3,2,8,32]{3,2,1,0:T(8,128)S(1)}, f32[3,2,8,32]{3,2,1,0:T(8,128)S(1)}, u32[]{:S(2)}, u32[]{:S(2)}) %collective-permute-start.17) | collective-permute-done | bytes 6176 | tf_op jit(solution)/shard_map/ppermute | solution.py:32
  163.7 1.3 collective-permute-start.18
  165.0 1.5 collective-permute-start.19
  166.5 1.6 collective-permute-done.19
  168.1 0.5 fusion.64
  168.6 1.4 convolution_bitcast_fusion
  170.0 6.1 %fusion.3 = f32[32,64,256]{2,0,1:T(8,128)S(1)} fusion(f32[3,8,64,256]{3,2,1,0:T(8,128)S(1)} %convolution_bitcast_fusion, f32[32]{0:T(128)S(1)} %get-tuple-element.202, s32[32]{0:T(128)S(1)} %get-tuple-element.207, f32[32]{0:T(128)S(1)} %get-tuple-element.194, s32[32]{0:T(128)S(1)} %get-tuple-element.209, f32[32]{0:T(128)S(1)} %get-tuple-element.201, ...), kind=kOutput, calls=%fused_computation.14 | convolution fusion | flops 158337792 | bytes 6816768 | tf_op jit(solution)/shard_map/za,cayx->czyx/dot_general | solution.py:62
  176.1 4.1 %fusion.39 = f32[3,8,64,256]{3,1,2,0:T(8,128)S(1)} fusion(f32[32,64,256]{2,0,1:T(8,128)S(1)} %fusion.3, f32[32]{0:T(128)S(1)} %get-tuple-element.202, s32[32]{0:T(128)S(1)} %get-tuple-element.207, f32[32]{0:T(128)S(1)} %get-tuple-element.194, s32[32]{0:T(128)S(1)} %get-tuple-element.209, f32[32]{0:T(128)S(1)} %get-tuple-element.201, ...), kind=kOutput, calls=%fused_computation.61 | convolution fusion | flops 157289216 | bytes 6816768 | tf_op jit(solution)/shard_map/za,czyx->cayx/dot_general | solution.py:67
  180.2 1.3 fusion.48
  181.6 0.5 fusion.80
  182.1 1.3 collective-permute-start.20
  183.4 4.5 %collective-permute-start.21 = (f32[3,2,12,32]{3,2,1,0:T(8,128)S(1)}, f32[3,2,12,32]{3,2,1,0:T(8,128)S(1)}, u32[]{:S(2)}, u32[]{:S(2)}) collective-permute-start(f32[3,2,12,32]{3,2,1,0:T(8,128)S(1)} %get-tuple-element.165), channel_id=1, source_target_pairs={{0,8},{8,16},{16,24},{1,9},{9,17},{17,25},{2,10},{10,18},{18,26},{... | collective-permute-start | bytes 27656 | tf_op jit(solution)/shard_map/ppermute | solution.py:19
  187.9 0.5 collective-permute-done.20
  188.4 1.2 collective-permute-done.21
  189.7 1.3 collective-permute-start.22
  191.0 3.0 %collective-permute-start.23 = (f32[3,4,2,32]{3,2,1,0:T(2,128)S(1)}, f32[3,4,2,32]{3,2,1,0:T(2,128)S(1)}, u32[]{:S(2)}, u32[]{:S(2)}) collective-permute-start(f32[3,4,2,32]{3,2,1,0:T(2,128)S(1)} %get-tuple-element.173), channel_id=1, source_target_pairs={{0,1},{1,2},{2,3},{3,4},{4,5},{5,6},{6,7},{8,9},{9,10},{10,11},{11... | collective-permute-start | bytes 9224 | tf_op jit(solution)/shard_map/ppermute | solution.py:19
  194.1 0.8 collective-permute-done.23
  194.9 0.6 multiply_reduce_fusion
  195.5 15.9 %all-reduce.1 = (f32[]{:T(128)}, f32[]{:T(128)}) all-reduce(f32[]{:T(128)} %get-tuple-element.147, f32[]{:T(128)} %get-tuple-element.146), channel_id=1, replica_groups=mesh['gz'=4,'gy'=8] {'gy'}, use_global_device_ids=true, to_apply=%region_8.9 | all-reduce | flops 2 | bytes 16 | tf_op jit(solution)/shard_map/psum | solution.py:12
  211.5 11.1 %all-reduce.3 = (f32[]{:T(128)}, f32[]{:T(128)}) all-reduce(f32[]{:T(128)} %get-tuple-element.150, f32[]{:T(128)} %get-tuple-element.151), channel_id=1, replica_groups=mesh['gz'=4,'gy'=8] {'gz'}, use_global_device_ids=true, to_apply=%region_9.10 | all-reduce | flops 2 | bytes 16 | tf_op jit(solution)/shard_map/psum | solution.py:13
  227.0 0.7 multiply_subtract_fusion
  (66 shorter events, 2.1 us)
Async XLA Ops:
  5.5 16.0 %collective-permute-start = (f32[2,3,64,256]{3,1,2,0:T(4,128)S(1)}, f32[2,3,64,256]{3,1,2,0:T(4,128)S(1)}, u32[]{:S(2)}, u32[]{:S(2)}) collective-permute-start(f32[2,3,64,256]{3,1,2,0:T(4,128)S(1)} %get-tuple-element.160), channel_id=1, source_target_pairs={{0,8},{8,16},{16,24},{1,9},{9,17},{17,25},{2,10},{10,18},{18,26},{... | collective-permute-start | bytes 1179656 | tf_op jit(solution)/shard_map/ppermute | solution.py:30
  10.4 24.3 %collective-permute-start.1 = (f32[2,3,64,256]{3,1,2,0:T(4,128)S(1)}, f32[2,3,64,256]{3,1,2,0:T(4,128)S(1)}, u32[]{:S(2)}, u32[]{:S(2)}) collective-permute-start(f32[2,3,64,256]{3,1,2,0:T(4,128)S(1)} %get-tuple-element.161), channel_id=1, source_target_pairs={{8,0},{16,8},{24,16},{9,1},{17,9},{25,17},{10,2},{18,10},{26,18},{... | collective-permute-start | bytes 1179656 | tf_op jit(solution)/shard_map/ppermute | solution.py:32
  11.8 26.1 %copy-start.3 = (f32[32,64,256]{2,1,0:T(8,128)S(1)}, f32[32,64,256]{2,1,0:T(8,128)}, u32[]{:S(2)}) copy-start(f32[32,64,256]{2,1,0:T(8,128)} %param.27) | copy-start | bytes 6291460
  11.8 26.0 %copy-start.4 = (f32[32,64,256]{2,1,0:T(8,128)S(1)}, f32[32,64,256]{2,1,0:T(8,128)}, u32[]{:S(2)}) copy-start(f32[32,64,256]{2,1,0:T(8,128)} %param.26) | copy-start | bytes 6291460
  34.8 6.1 %collective-permute-start.2 = (f32[2,38,3,256]{3,1,2,0:T(8,128)S(1)}, f32[2,38,3,256]{3,1,2,0:T(8,128)S(1)}, u32[]{:S(2)}, u32[]{:S(2)}) collective-permute-start(f32[2,38,3,256]{3,1,2,0:T(8,128)S(1)} %get-tuple-element.158), channel_id=1, source_target_pairs={{0,1},{1,2},{2,3},{3,4},{4,5},{5,6},{6,7},{8,9},{9,10},{10,11},{11... | collective-permute-start | bytes 700424 | tf_op jit(solution)/shard_map/ppermute | solution.py:30
  36.1 5.2 %collective-permute-start.3 = (f32[2,38,3,256]{3,1,2,0:T(8,128)S(1)}, f32[2,38,3,256]{3,1,2,0:T(8,128)S(1)}, u32[]{:S(2)}, u32[]{:S(2)}) collective-permute-start(f32[2,38,3,256]{3,1,2,0:T(8,128)S(1)} %get-tuple-element.159), channel_id=1, source_target_pairs={{1,0},{2,1},{3,2},{4,3},{5,4},{6,5},{7,6},{9,8},{10,9},{11,10},{12... | collective-permute-start | bytes 700424 | tf_op jit(solution)/shard_map/ppermute | solution.py:32
  58.4 37.9 %copy-start = (bf16[1,32,64,256]{3,1,2,0:T(8,128)(2,1)S(1)}, bf16[1,32,64,256]{3,1,2,0:T(8,128)(2,1)}, u32[]{:S(2)}) copy-start(bf16[1,32,64,256]{3,1,2,0:T(8,128)(2,1)} %get-tuple-element.162) | copy-start | bytes 3145732
  58.5 37.9 %copy-start.1 = (bf16[1,32,64,256]{3,1,2,0:T(8,128)(2,1)S(1)}, bf16[1,32,64,256]{3,1,2,0:T(8,128)(2,1)}, u32[]{:S(2)}) copy-start(bf16[1,32,64,256]{3,1,2,0:T(8,128)(2,1)} %get-tuple-element.163) | copy-start | bytes 3145732
  58.5 37.9 %copy-start.2 = (bf16[1,32,64,256]{3,1,2,0:T(8,128)(2,1)S(1)}, bf16[1,32,64,256]{3,1,2,0:T(8,128)(2,1)}, u32[]{:S(2)}) copy-start(bf16[1,32,64,256]{3,1,2,0:T(8,128)(2,1)} %get-tuple-element.164) | copy-start | bytes 3145732
  59.0 6.1 %collective-permute-start.4 = (f32[3,2,12,32]{3,2,1,0:T(8,128)S(1)}, f32[3,2,12,32]{3,2,1,0:T(8,128)S(1)}, u32[]{:S(2)}, u32[]{:S(2)}) collective-permute-start(f32[3,2,12,32]{3,2,1,0:T(8,128)S(1)} %get-tuple-element.170), channel_id=1, source_target_pairs={{8,0},{16,8},{24,16},{9,1},{17,9},{25,17},{10,2},{18,10},{26,18},{... | collective-permute-start | bytes 27656 | tf_op jit(solution)/shard_map/ppermute | solution.py:19
  60.4 6.3 %collective-permute-start.5 = (f32[3,2,12,32]{3,2,1,0:T(8,128)S(1)}, f32[3,2,12,32]{3,2,1,0:T(8,128)S(1)}, u32[]{:S(2)}, u32[]{:S(2)}) collective-permute-start(f32[3,2,12,32]{3,2,1,0:T(8,128)S(1)} %get-tuple-element.169), channel_id=1, source_target_pairs={{0,8},{8,16},{16,24},{1,9},{9,17},{17,25},{2,10},{10,18},{18,26},{... | collective-permute-start | bytes 27656 | tf_op jit(solution)/shard_map/ppermute | solution.py:19
  66.7 7.5 %collective-permute-start.6 = (f32[3,4,2,32]{3,2,1,0:T(2,128)S(1)}, f32[3,4,2,32]{3,2,1,0:T(2,128)S(1)}, u32[]{:S(2)}, u32[]{:S(2)}) collective-permute-start(f32[3,4,2,32]{3,2,1,0:T(2,128)S(1)} %get-tuple-element.182), channel_id=1, source_target_pairs={{1,0},{2,1},{3,2},{4,3},{5,4},{6,5},{7,6},{9,8},{10,9},{11,10},{12... | collective-permute-start | bytes 9224 | tf_op jit(solution)/shard_map/ppermute | solution.py:19
  68.1 6.8 %collective-permute-start.7 = (f32[3,4,2,32]{3,2,1,0:T(2,128)S(1)}, f32[3,4,2,32]{3,2,1,0:T(2,128)S(1)}, u32[]{:S(2)}, u32[]{:S(2)}) collective-permute-start(f32[3,4,2,32]{3,2,1,0:T(2,128)S(1)} %get-tuple-element.181), channel_id=1, source_target_pairs={{0,1},{1,2},{2,3},{3,4},{4,5},{5,6},{6,7},{8,9},{9,10},{10,11},{11... | collective-permute-start | bytes 9224 | tf_op jit(solution)/shard_map/ppermute | solution.py:19
  74.9 5.8 %collective-permute-start.8 = (f32[3,2,8,32]{3,2,1,0:T(8,128)S(1)}, f32[3,2,8,32]{3,2,1,0:T(8,128)S(1)}, u32[]{:S(2)}, u32[]{:S(2)}) collective-permute-start(f32[3,2,8,32]{3,2,1,0:T(8,128)S(1)} %get-tuple-element.185), channel_id=1, source_target_pairs={{0,8},{8,16},{16,24},{1,9},{9,17},{17,25},{2,10},{10,18},{18,26},{... | collective-permute-start | bytes 18440 | tf_op jit(solution)/shard_map/ppermute | solution.py:30
  79.2 6.7 %collective-permute-start.9 = (f32[3,2,8,32]{3,2,1,0:T(8,128)S(1)}, f32[3,2,8,32]{3,2,1,0:T(8,128)S(1)}, u32[]{:S(2)}, u32[]{:S(2)}) collective-permute-start(f32[3,2,8,32]{3,2,1,0:T(8,128)S(1)} %get-tuple-element.186), channel_id=1, source_target_pairs={{8,0},{16,8},{24,16},{9,1},{17,9},{25,17},{10,2},{18,10},{26,18},{... | collective-permute-start | bytes 18440 | tf_op jit(solution)/shard_map/ppermute | solution.py:32
  85.9 3.8 %collective-permute-start.10 = (f32[3,8,2,32]{3,2,1,0:T(2,128)S(1)}, f32[3,8,2,32]{3,2,1,0:T(2,128)S(1)}, u32[]{:S(2)}, u32[]{:S(2)}) collective-permute-start(f32[3,8,2,32]{3,2,1,0:T(2,128)S(1)} %get-tuple-element.179), channel_id=1, source_target_pairs={{0,1},{1,2},{2,3},{3,4},{4,5},{5,6},{6,7},{8,9},{9,10},{10,11},{11... | collective-permute-start | bytes 18440 | tf_op jit(solution)/shard_map/ppermute | solution.py:30
  88.4 6.0 %collective-permute-start.11 = (f32[3,8,2,32]{3,2,1,0:T(2,128)S(1)}, f32[3,8,2,32]{3,2,1,0:T(2,128)S(1)}, u32[]{:S(2)}, u32[]{:S(2)}) collective-permute-start(f32[3,8,2,32]{3,2,1,0:T(2,128)S(1)} %get-tuple-element.180), channel_id=1, source_target_pairs={{1,0},{2,1},{3,2},{4,3},{5,4},{6,5},{7,6},{9,8},{10,9},{11,10},{12... | collective-permute-start | bytes 18440 | tf_op jit(solution)/shard_map/ppermute | solution.py:32
  108.4 6.9 %collective-permute-start.12 = (f32[3,2,12,32]{3,2,1,0:T(8,128)S(1)}, f32[3,2,12,32]{3,2,1,0:T(8,128)S(1)}, u32[]{:S(2)}, u32[]{:S(2)}) collective-permute-start(f32[3,2,12,32]{3,2,1,0:T(8,128)S(1)} %get-tuple-element.168), channel_id=1, source_target_pairs={{8,0},{16,8},{24,16},{9,1},{17,9},{25,17},{10,2},{18,10},{26,18},{... | collective-permute-start | bytes 27656 | tf_op jit(solution)/shard_map/ppermute | solution.py:19
  109.7 7.2 %collective-permute-start.13 = (f32[3,2,12,32]{3,2,1,0:T(8,128)S(1)}, f32[3,2,12,32]{3,2,1,0:T(8,128)S(1)}, u32[]{:S(2)}, u32[]{:S(2)}) collective-permute-start(f32[3,2,12,32]{3,2,1,0:T(8,128)S(1)} %get-tuple-element.167), channel_id=1, source_target_pairs={{0,8},{8,16},{16,24},{1,9},{9,17},{17,25},{2,10},{10,18},{18,26},{... | collective-permute-start | bytes 27656 | tf_op jit(solution)/shard_map/ppermute | solution.py:19
  116.9 5.6 %collective-permute-start.14 = (f32[3,4,2,32]{3,2,1,0:T(2,128)S(1)}, f32[3,4,2,32]{3,2,1,0:T(2,128)S(1)}, u32[]{:S(2)}, u32[]{:S(2)}) collective-permute-start(f32[3,4,2,32]{3,2,1,0:T(2,128)S(1)} %get-tuple-element.178), channel_id=1, source_target_pairs={{1,0},{2,1},{3,2},{4,3},{5,4},{6,5},{7,6},{9,8},{10,9},{11,10},{12... | collective-permute-start | bytes 9224 | tf_op jit(solution)/shard_map/ppermute | solution.py:19
  118.3 5.1 %collective-permute-start.15 = (f32[3,4,2,32]{3,2,1,0:T(2,128)S(1)}, f32[3,4,2,32]{3,2,1,0:T(2,128)S(1)}, u32[]{:S(2)}, u32[]{:S(2)}) collective-permute-start(f32[3,4,2,32]{3,2,1,0:T(2,128)S(1)} %get-tuple-element.177), channel_id=1, source_target_pairs={{0,1},{1,2},{2,3},{3,4},{4,5},{5,6},{6,7},{8,9},{9,10},{10,11},{11... | collective-permute-start | bytes 9224 | tf_op jit(solution)/shard_map/ppermute | solution.py:19
  154.1 5.3 %collective-permute-start.16 = (f32[3,2,8,32]{3,2,1,0:T(8,128)S(1)}, f32[3,2,8,32]{3,2,1,0:T(8,128)S(1)}, u32[]{:S(2)}, u32[]{:S(2)}) collective-permute-start(f32[3,2,8,32]{3,2,1,0:T(8,128)S(1)} %get-tuple-element.183), channel_id=1, source_target_pairs={{0,8},{8,16},{16,24},{1,9},{9,17},{17,25},{2,10},{10,18},{18,26},{... | collective-permute-start | bytes 18440 | tf_op jit(solution)/shard_map/ppermute | solution.py:30
  158.0 5.7 %collective-permute-start.17 = (f32[3,2,8,32]{3,2,1,0:T(8,128)S(1)}, f32[3,2,8,32]{3,2,1,0:T(8,128)S(1)}, u32[]{:S(2)}, u32[]{:S(2)}) collective-permute-start(f32[3,2,8,32]{3,2,1,0:T(8,128)S(1)} %get-tuple-element.184), channel_id=1, source_target_pairs={{8,0},{16,8},{24,16},{9,1},{17,9},{25,17},{10,2},{18,10},{26,18},{... | collective-permute-start | bytes 18440 | tf_op jit(solution)/shard_map/ppermute | solution.py:32
  163.7 2.8 %collective-permute-start.18 = (f32[3,8,2,32]{3,2,1,0:T(2,128)S(1)}, f32[3,8,2,32]{3,2,1,0:T(2,128)S(1)}, u32[]{:S(2)}, u32[]{:S(2)}) collective-permute-start(f32[3,8,2,32]{3,2,1,0:T(2,128)S(1)} %get-tuple-element.175), channel_id=1, source_target_pairs={{0,1},{1,2},{2,3},{3,4},{4,5},{5,6},{6,7},{8,9},{9,10},{10,11},{11... | collective-permute-start | bytes 18440 | tf_op jit(solution)/shard_map/ppermute | solution.py:30
  165.0 3.1 %collective-permute-start.19 = (f32[3,8,2,32]{3,2,1,0:T(2,128)S(1)}, f32[3,8,2,32]{3,2,1,0:T(2,128)S(1)}, u32[]{:S(2)}, u32[]{:S(2)}) collective-permute-start(f32[3,8,2,32]{3,2,1,0:T(2,128)S(1)} %get-tuple-element.176), channel_id=1, source_target_pairs={{1,0},{2,1},{3,2},{4,3},{5,4},{6,5},{7,6},{9,8},{10,9},{11,10},{12... | collective-permute-start | bytes 18440 | tf_op jit(solution)/shard_map/ppermute | solution.py:32
  182.1 6.4 %collective-permute-start.20 = (f32[3,2,12,32]{3,2,1,0:T(8,128)S(1)}, f32[3,2,12,32]{3,2,1,0:T(8,128)S(1)}, u32[]{:S(2)}, u32[]{:S(2)}) collective-permute-start(f32[3,2,12,32]{3,2,1,0:T(8,128)S(1)} %get-tuple-element.166), channel_id=1, source_target_pairs={{8,0},{16,8},{24,16},{9,1},{17,9},{25,17},{10,2},{18,10},{26,18},{... | collective-permute-start | bytes 27656 | tf_op jit(solution)/shard_map/ppermute | solution.py:19
  183.4 6.3 %collective-permute-start.21 = (f32[3,2,12,32]{3,2,1,0:T(8,128)S(1)}, f32[3,2,12,32]{3,2,1,0:T(8,128)S(1)}, u32[]{:S(2)}, u32[]{:S(2)}) collective-permute-start(f32[3,2,12,32]{3,2,1,0:T(8,128)S(1)} %get-tuple-element.165), channel_id=1, source_target_pairs={{0,8},{8,16},{16,24},{1,9},{9,17},{17,25},{2,10},{10,18},{18,26},{... | collective-permute-start | bytes 27656 | tf_op jit(solution)/shard_map/ppermute | solution.py:19
  189.7 4.4 %collective-permute-start.22 = (f32[3,4,2,32]{3,2,1,0:T(2,128)S(1)}, f32[3,4,2,32]{3,2,1,0:T(2,128)S(1)}, u32[]{:S(2)}, u32[]{:S(2)}) collective-permute-start(f32[3,4,2,32]{3,2,1,0:T(2,128)S(1)} %get-tuple-element.174), channel_id=1, source_target_pairs={{1,0},{2,1},{3,2},{4,3},{5,4},{6,5},{7,6},{9,8},{10,9},{11,10},{12... | collective-permute-start | bytes 9224 | tf_op jit(solution)/shard_map/ppermute | solution.py:19
  191.0 3.9 %collective-permute-start.23 = (f32[3,4,2,32]{3,2,1,0:T(2,128)S(1)}, f32[3,4,2,32]{3,2,1,0:T(2,128)S(1)}, u32[]{:S(2)}, u32[]{:S(2)}) collective-permute-start(f32[3,4,2,32]{3,2,1,0:T(2,128)S(1)} %get-tuple-element.173), channel_id=1, source_target_pairs={{0,1},{1,2},{2,3},{3,4},{4,5},{5,6},{6,7},{8,9},{9,10},{10,11},{11... | collective-permute-start | bytes 9224 | tf_op jit(solution)/shard_map/ppermute | solution.py:19
